TPU v7x, 32 devices: a whole 2x2x4 slice. The times are simulated.
32 devices in a mesh: role: 4 (over y, x), dom: 8 (over z, core).
Axes of the slice: x: 2, y: 2, z: 4, core: 2. Of those that a mesh axis runs over, the one named last changes fastest.
Arguments:
- node_feats: bfloat16 [4096, 512], P(('role', 'dom')), may hold values from -6 to 6
- hub_feats: bfloat16 [128, 512], P(('role', 'dom')), may hold values from -6 to 6
- weight: bfloat16 [1024, 512], replicated, may hold values from -0.1875 to 0.1875
- edge_src: int32 [32, 1024], P(('role', 'dom')), may hold values from 0 to 287, as said below
- edge_dst: int32 [32, 1024], P(('role', 'dom')), may hold values from 0 to 127, as said below
- bound_rows: int32 [32, 16], P(('role', 'dom')), may hold values from 0 to 127
- hub_edge_src: int32 [32, 128], P(('role', 'dom')), may hold values from 0 to 127
- hub_edge_slot: int32 [32, 128], P(('role', 'dom')), may hold values from 0 to 63, as said below
- slot_hub: int32 [32, 64], P(('role', 'dom')), may hold values from 0 to 3, as said below
Outputs:
- node_out: bfloat16 [4096, 512], P(('role', 'dom'))
- hub_out: bfloat16 [128, 512], P(('role', 'dom'))
Inputs may be any that keep to these rules, and one draw needn't show every extreme that they name: `edge_src`: row indices into the source table of the device: its own nodes, then 16 rows of the device before it along dom, then 16 of the device after it, then the 128 hubs. `edge_dst`: each node of a device is the destination of at least one of the device's edges. `hub_edge_slot`: every slot of a device receives at least one of its hub edges; slot s belongs to the owner numbered s // 2. `slot_hub`: every hub of every owner is fed by at least one slot of some device.
All inputs are finite; a program needn't handle non-finite values.
Results may differ from a plain program's by a relative error of at most 0.0027.
Values may be sent and summed in bfloat16 or wider, within the bound.
A program may use at most 64 MiB of HBM per device.

v0:
```python
import math
import jax
import jax.numpy as jnp
from jax import lax
from jax.sharding import PartitionSpec as P

epsilon = 1e-06


def extended(block, sides, width):
    for axis, dim in sides:
        count = lax.axis_size(axis)
        forward = [(i, i + 1) for i in range(count - 1)]
        forward.append((count - 1, 0))
        backward = [(target, source) for source, target in forward]
        low = lax.ppermute(
            lax.slice_in_dim(block, block.shape[dim] - width, None, axis=dim), axis, forward
        )
        high = lax.ppermute(lax.slice_in_dim(block, 0, width, axis=dim), axis, backward)
        block = jnp.concatenate([low, block, high], axis=dim)
    return block


def sage_update(self_rows, mean_rows, weight):
    feature_width = self_rows.shape[1]
    linear = jnp.dot(self_rows, weight[:feature_width], preferred_element_type=jnp.float32)
    linear = linear + jnp.dot(mean_rows, weight[feature_width:], preferred_element_type=jnp.float32)
    rectified = jnp.maximum(linear, 0.0)
    inverse_norm = lax.rsqrt(jnp.mean(rectified * rectified, axis=1, keepdims=True) + epsilon)
    return (rectified * inverse_norm).astype(jnp.bfloat16)


def on_device(
    node_feats,
    hub_feats,
    weight,
    edge_src,
    edge_dst,
    bound_rows,
    hub_edge_src,
    hub_edge_slot,
    slot_hub,
):
    feature_width = node_feats.shape[1]
    local_nodes = node_feats.shape[0]
    hub_local = hub_feats.shape[0]
    exports = node_feats[bound_rows[0]]
    bound_size = exports.shape[0]
    widened = extended(exports, (("dom", 0),), bound_size)
    hub_table = lax.all_gather(hub_feats, ("role", "dom"), axis=0, tiled=True)
    source_table = jnp.concatenate(
        [node_feats, widened[:bound_size], widened[2 * bound_size :], hub_table], axis=0
    )
    sources = edge_src[0]
    targets = edge_dst[0]
    edge_block = math.gcd(sources.shape[0], 2048)

    def add_block(sums, indices):
        node_sums, node_degree = sums
        block_sources, block_targets = indices
        picked = source_table[block_sources].astype(jnp.float32)
        return (
            (node_sums.at[block_targets].add(picked), node_degree.at[block_targets].add(1.0)),
            None,
        )

    initial = (
        jnp.zeros((local_nodes, feature_width), jnp.float32),
        jnp.zeros((local_nodes,), jnp.float32),
    )
    (node_sums, node_degree), unused = lax.scan(
        add_block, initial, (sources.reshape(-1, edge_block), targets.reshape(-1, edge_block))
    )
    hub_sources = hub_edge_src[0]
    hub_slots = hub_edge_slot[0]
    slot_table = slot_hub[0]
    slot_total = slot_table.shape[0]
    role_count = lax.axis_size("role")
    dom_count = lax.axis_size("dom")
    per_owner = slot_total // (role_count * dom_count)
    partial_value = (
        jnp.zeros((slot_total, feature_width), jnp.float32)
        .at[hub_slots]
        .add(node_feats[hub_sources].astype(jnp.float32))
    )
    slot_counts = jnp.zeros((slot_total,), jnp.float32).at[hub_slots].add(1.0)
    outgoing = (
        partial_value.reshape(role_count, dom_count, per_owner, feature_width),
        slot_counts.reshape(role_count, dom_count, per_owner),
        slot_table.astype(jnp.float32).reshape(role_count, dom_count, per_owner),
    )
    incoming_rows, incoming_counts, incoming_hubs = (
        lax.all_to_all(
            lax.all_to_all(outgoing[0], "role", split_axis=0, concat_axis=0, tiled=True),
            "dom",
            split_axis=1,
            concat_axis=1,
            tiled=True,
        ),
        lax.all_to_all(
            lax.all_to_all(outgoing[1], "role", split_axis=0, concat_axis=0, tiled=True),
            "dom",
            split_axis=1,
            concat_axis=1,
            tiled=True,
        ),
        lax.all_to_all(
            lax.all_to_all(outgoing[2], "role", split_axis=0, concat_axis=0, tiled=True),
            "dom",
            split_axis=1,
            concat_axis=1,
            tiled=True,
        ),
    )
    incoming_rows = incoming_rows.reshape(-1, feature_width)
    onehot = (
        incoming_hubs.reshape(-1)[:, None] == jnp.arange(hub_local, dtype=jnp.float32)[None, :]
    ).astype(jnp.float32)
    hub_sums = jnp.dot(
        onehot.T, incoming_rows, precision=lax.Precision.HIGHEST, preferred_element_type=jnp.float32
    )
    hub_degree = jnp.dot(
        incoming_counts.reshape(-1),
        onehot,
        precision=lax.Precision.HIGHEST,
        preferred_element_type=jnp.float32,
    )
    node_mean = (node_sums / node_degree[:, None]).astype(jnp.bfloat16)
    node_out = sage_update(node_feats, node_mean, weight)
    hub_mean = (hub_sums / hub_degree[:, None]).astype(jnp.bfloat16)
    hub_out = sage_update(hub_feats, hub_mean, weight)
    return (node_out, hub_out)


def solution(mesh):
    return jax.shard_map(
        on_device,
        mesh=mesh,
        in_specs=(
            P(("role", "dom"), None),
            P(("role", "dom"), None),
            P(),
            P(("role", "dom"), None),
            P(("role", "dom"), None),
            P(("role", "dom"), None),
            P(("role", "dom"), None),
            P(("role", "dom"), None),
            P(("role", "dom"), None),
        ),
        out_specs=(P(("role", "dom"), None), P(("role", "dom"), None)),
        check_vma=False,
    )
```

profile of v0, /device:TPU:0, one launch (start us, length us, event | category | flops | bytes accessed | tf_op | source)
XLA Modules:
  0.0 118.5 jit_solution(10749074931665273671)
XLA Ops:
  0.6 0.0 copy-start
  0.6 0.0 copy-start.1
  0.7 0.0 copy-start.2
  0.7 0.0 copy-start.3
  0.7 0.0 copy-start.4
  0.7 0.0 copy-start.5
  0.7 0.0 copy-start.6
  0.7 0.7 fusion.18
  1.5 1.5 %gather_fusion = bf16[16,512]{1,0:T(8,128)(2,1)S(1)} fusion(bf16[128,512]{1,0:T(8,128)(2,1)} %param.9, s32[1024]{0:T(1024)S(1)} %pad_clamp_fusion.1), kind=kCustom, calls=%fused_computation | custom fusion | bytes 32832 | tf_op jit(solution)/shard_map/gather | solution.py:47
  3.0 0.5 collective-permute-start
  3.5 4.1 %collective-permute-start.1 = (bf16[16,512]{1,0:T(8,128)(2,1)S(1)}, bf16[16,512]{1,0:T(8,128)(2,1)S(1)}, u32[]{:S(2)}, u32[]{:S(2)}) collective-permute-start(bf16[16,512]{1,0:T(8,128)(2,1)S(1)} %gather_fusion), channel_id=1, source_target_pairs={{1,0},{2,1},{3,2},{4,3},{5,4},{6,5},{7,6},{0,7},{9,8},{10,9},{11,1... | collective-permute-start | bytes 49160 | tf_op jit(solution)/shard_map/ppermute | solution.py:19
  7.6 0.7 fusion.19
  8.3 1.4 %scatter_custom_fusion.3 = f32[64]{0:T(128)S(1)} fusion(s32[128]{0:T(128)S(1)} %fusion.19, f32[128]{0:T(128)S(1)} %broadcast.143, f32[]{:T(128)} %constant.9.clone.1), kind=kCustom, calls=%fused_computation.50 | custom fusion | flops 128 | bytes 260 | tf_op jit(solution)/shard_map/scatter-add | solution.py:86
  9.7 0.1 reshape.180
  9.8 0.7 copy.22
  10.5 4.2 %all-to-all-start.4 = ((f32[4,8,2]{1,2,0:T(2,128)}), f32[4,8,2]{1,2,0:T(2,128)S(1)}, u32[]{:S(2)}, u32[]{:S(2)}) async-start(f32[4,8,2]{1,2,0:T(2,128)} %copy.22), calls=%async_computation.4 | async-start | bytes 8192 | tf_op jit(solution)/shard_map/all_to_all | solution.py:101
  14.6 1.3 %fusion.9 = f32[128,512]{1,0:T(8,128)S(1)} fusion(bf16[128,512]{1,0:T(8,128)(2,1)} %param.9, bf16[1024,512]{1,0:T(8,128)(2,1)} %param.11), kind=kOutput, calls=%fused_computation.20 | convolution fusion | flops 67108864 | bytes 917504 | tf_op jit(solution)/shard_map/dot_general | solution.py:26
  16.0 0.0 copy-done
  16.0 0.9 fusion.7
  16.9 0.0 copy-done.3
  16.9 0.0 copy-done.4
  16.9 0.0 copy-done.5
  16.9 0.1 convert_element_type.31
  17.1 0.7 copy.17
  17.7 1.6 %all-to-all-done.4 = f32[4,8,2]{1,2,0:T(2,128)S(1)} async-done(((f32[4,8,2]{1,2,0:T(2,128)}), f32[4,8,2]{1,2,0:T(2,128)S(1)}, u32[]{:S(2)}, u32[]{:S(2)}) %all-to-all-start.4) | async-done | bytes 288 | tf_op jit(solution)/shard_map/all_to_all | solution.py:101
  19.3 3.2 %all-to-all-start = ((f32[4,8,2]{1,2,0:T(2,128)}), f32[4,8,2]{1,2,0:T(2,128)S(1)}, u32[]{:S(2)}, u32[]{:S(2)}) async-start(f32[4,8,2]{1,2,0:T(2,128)} %copy.17), calls=%async_computation | async-start | bytes 8192 | tf_op jit(solution)/shard_map/all_to_all | solution.py:108
  22.6 0.0 copy-done.6
  22.6 0.7 copy.23
  23.3 3.9 %all-to-all-done = f32[4,8,2]{1,2,0:T(2,128)S(1)} async-done(((f32[4,8,2]{1,2,0:T(2,128)}), f32[4,8,2]{1,2,0:T(2,128)S(1)}, u32[]{:S(2)}, u32[]{:S(2)}) %all-to-all-start) | async-done | bytes 288 | tf_op jit(solution)/shard_map/all_to_all | solution.py:108
  27.2 3.3 %all-to-all-start.5 = ((f32[4,8,2]{0,2,1:T(2,128)}), f32[4,8,2]{0,2,1:T(2,128)S(1)}, u32[]{:S(2)}, u32[]{:S(2)}) async-start(f32[4,8,2]{0,2,1:T(2,128)} %copy.23), calls=%async_computation.5 | async-start | bytes 16384 | tf_op jit(solution)/shard_map/all_to_all | solution.py:100
  30.6 0.7 copy.18
  31.3 4.8 %all-to-all-done.5 = f32[4,8,2]{0,2,1:T(2,128)S(1)} async-done(((f32[4,8,2]{0,2,1:T(2,128)}), f32[4,8,2]{0,2,1:T(2,128)S(1)}, u32[]{:S(2)}, u32[]{:S(2)}) %all-to-all-start.5) | async-done | bytes 288 | tf_op jit(solution)/shard_map/all_to_all | solution.py:100
  36.1 3.3 %all-to-all-start.1 = ((f32[4,8,2]{0,2,1:T(2,128)}), f32[4,8,2]{0,2,1:T(2,128)S(1)}, u32[]{:S(2)}, u32[]{:S(2)}) async-start(f32[4,8,2]{0,2,1:T(2,128)} %copy.18), calls=%async_computation.1 | async-start | bytes 16384 | tf_op jit(solution)/shard_map/all_to_all | solution.py:107
  39.4 0.0 copy-done.2
  39.4 40.5 %all-gather = bf16[32,4,512]{2,1,0:T(4,128)(2,1)S(1)} all-gather(bf16[1,4,512]{2,1,0:T(4,128)(2,1)S(1)} %bitcast.26), channel_id=1, replica_groups=mesh['role'=4,'dom'=8] {'role','dom'}, dimensions={0}, use_global_device_ids=true | all-gather | bytes 135168 | tf_op jit(solution)/shard_map/all_gather | solution.py:50
  80.0 0.0 copy-done.1
  80.0 2.0 %scatter_custom_fusion.2 = f32[64,512]{1,0:T(8,128)S(1)} fusion(s32[128]{0:T(128)S(1)} %fusion.19, f32[]{:T(128)} %constant.9.clone.1, bf16[128,512]{1,0:T(8,128)(2,1)S(1)} %copy-done.1, s32[1024]{0:T(1024)S(1)} %pad_clamp_fusion), kind=kCustom, calls=%fused_computation.23 | custom fusion | flops 131072 | bytes 266244 | tf_op jit(solution)/shard_map/scatter-add | solution.py:84
  81.9 0.7 reshape.178
  82.7 7.6 %scatter_custom_fusion.1 = f32[128]{0:T(128)S(1)} fusion(s32[1024]{0:T(1024)S(1)} %bitcast.28, f32[1024]{0:T(1024)S(1)} %broadcast.142, f32[]{:T(128)} %constant.9.clone.1), kind=kCustom, calls=%fused_computation.52 | custom fusion | flops 1024 | bytes 516 | tf_op jit(solution)/shard_map/while/body/eval_jaxpr/scatter-add | solution.py:63
  90.3 0.1 copy.24
  90.5 0.1 reshape.240
  90.6 0.0 all-to-all-done.1
  90.6 3.3 %all-to-all-start.2 = ((f32[4,8,2,512]{3,2,1,0:T(2,128)}), f32[4,8,2,512]{3,2,1,0:T(2,128)S(1)}, u32[]{:S(2)}, u32[]{:S(2)}) async-start(f32[4,8,2,512]{3,2,1,0:T(2,128)} %reshape.178), calls=%async_computation.2 | async-start | bytes 262144 | tf_op jit(solution)/shard_map/all_to_all | solution.py:94
  93.9 0.1 copy.19
  94.1 0.1 eq.15
  94.2 0.2 convolution_bitcast_fusion
  94.4 0.0 collective-permute-done
  94.4 0.0 collective-permute-done.1
  94.4 11.6 %scatter_custom_fusion = f32[128,512]{1,0:T(8,128)S(1)} fusion(s32[1024]{0:T(1024)S(1)} %bitcast.29, f32[]{:T(128)} %constant.9.clone.1, bf16[288,512]{1,0:T(8,128)(2,1)S(1)} %pad_maximum_fusion, s32[1024]{0:T(1024)S(1)} %broadcast_clamp_fusion), kind=kCustom, calls=%fused_computation.7 | custom fusion | flops 1048576 | bytes 561156 | tf_op jit(solution)/shard_map/while/body/eval_jaxpr/scatter-add | solution.py:63
  106.0 0.4 multiply_reduce_fusion
  106.4 0.0 all-to-all-done.2
  106.4 0.7 copy.20
  107.0 3.4 %all-to-all-start.3 = ((f32[4,8,2,512]{3,2,0,1:T(2,128)}), f32[4,8,2,512]{3,2,0,1:T(2,128)S(1)}, u32[]{:S(2)}, u32[]{:S(2)}) async-start(f32[4,8,2,512]{3,2,0,1:T(2,128)} %copy.20), calls=%async_computation.3 | async-start | bytes 262144 | tf_op jit(solution)/shard_map/all_to_all | solution.py:93
  110.4 0.7 multiply_convert_fusion
  111.2 5.9 %all-to-all-done.3 = f32[4,8,2,512]{3,2,0,1:T(2,128)S(1)} async-done(((f32[4,8,2,512]{3,2,0,1:T(2,128)}), f32[4,8,2,512]{3,2,0,1:T(2,128)S(1)}, u32[]{:S(2)}, u32[]{:S(2)}) %all-to-all-start.3) | async-done | bytes 131104 | tf_op jit(solution)/shard_map/all_to_all | solution.py:93
  117.1 0.1 reshape.179
  117.2 0.3 fusion.4
  117.5 0.3 multiply_reduce_fusion.1
  117.8 0.7 multiply_convert_fusion.1
  (14 shorter events, 0.2 us)
Async XLA Ops:
  0.6 15.4 %copy-start = (bf16[1024,512]{1,0:T(8,128)(2,1)S(1)}, bf16[1024,512]{1,0:T(8,128)(2,1)}, u32[]{:S(2)}) copy-start(bf16[1024,512]{1,0:T(8,128)(2,1)} %param.11) | copy-start | bytes 3145732
  0.6 79.3 %copy-start.1 = (bf16[128,512]{1,0:T(8,128)(2,1)S(1)}, bf16[128,512]{1,0:T(8,128)(2,1)}, u32[]{:S(2)}) copy-start(bf16[128,512]{1,0:T(8,128)(2,1)} %param.9) | copy-start | bytes 393220
  0.7 38.8 %copy-start.2 = (bf16[4,512]{1,0:T(4,128)(2,1)S(1)}, bf16[4,512]{1,0:T(4,128)(2,1)}, u32[]{:S(2)}) copy-start(bf16[4,512]{1,0:T(4,128)(2,1)} %param.10) | copy-start | bytes 12292
  0.7 16.2 %copy-start.3 = (s32[1,1024]{1,0:T(1,128)S(1)}, s32[1,1024]{1,0:T(1,128)}, u32[]{:S(2)}) copy-start(s32[1,1024]{1,0:T(1,128)} %param.13) | copy-start | bytes 12292
  0.7 16.2 %copy-start.4 = (s32[1,1024]{1,0:T(1,128)S(1)}, s32[1,1024]{1,0:T(1,128)}, u32[]{:S(2)}) copy-start(s32[1,1024]{1,0:T(1,128)} %param.12) | copy-start | bytes 12292
  0.7 16.2 %copy-start.5 = (s32[1,64]{1,0:T(1,128)S(1)}, s32[1,64]{1,0:T(1,128)}, u32[]{:S(2)}) copy-start(s32[1,64]{1,0:T(1,128)} %param.17) | copy-start | bytes 772
  0.7 21.9 %copy-start.6 = (s32[1,128]{1,0:T(1,128)S(1)}, s32[1,128]{1,0:T(1,128)}, u32[]{:S(2)}) copy-start(s32[1,128]{1,0:T(1,128)} %param.15) | copy-start | bytes 1540
  3.0 91.4 %collective-permute-start = (bf16[16,512]{1,0:T(8,128)(2,1)S(1)}, bf16[16,512]{1,0:T(8,128)(2,1)S(1)}, u32[]{:S(2)}, u32[]{:S(2)}) collective-permute-start(bf16[16,512]{1,0:T(8,128)(2,1)S(1)} %gather_fusion), channel_id=1, source_target_pairs={{0,1},{1,2},{2,3},{3,4},{4,5},{5,6},{6,7},{7,0},{8,9},{9,10},{10,1... | collective-permute-start | bytes 49160 | tf_op jit(solution)/shard_map/ppermute | solution.py:16
  3.5 90.9 %collective-permute-start.1 = (bf16[16,512]{1,0:T(8,128)(2,1)S(1)}, bf16[16,512]{1,0:T(8,128)(2,1)S(1)}, u32[]{:S(2)}, u32[]{:S(2)}) collective-permute-start(bf16[16,512]{1,0:T(8,128)(2,1)S(1)} %gather_fusion), channel_id=1, source_target_pairs={{1,0},{2,1},{3,2},{4,3},{5,4},{6,5},{7,6},{0,7},{9,8},{10,9},{11,1... | collective-permute-start | bytes 49160 | tf_op jit(solution)/shard_map/ppermute | solution.py:19
  10.5 8.8 %all-to-all-start.4 = ((f32[4,8,2]{1,2,0:T(2,128)}), f32[4,8,2]{1,2,0:T(2,128)S(1)}, u32[]{:S(2)}, u32[]{:S(2)}) async-start(f32[4,8,2]{1,2,0:T(2,128)} %copy.22), calls=%async_computation.4 | async-start | bytes 8192 | tf_op jit(solution)/shard_map/all_to_all | solution.py:101
  19.3 7.9 %all-to-all-start = ((f32[4,8,2]{1,2,0:T(2,128)}), f32[4,8,2]{1,2,0:T(2,128)S(1)}, u32[]{:S(2)}, u32[]{:S(2)}) async-start(f32[4,8,2]{1,2,0:T(2,128)} %copy.17), calls=%async_computation | async-start | bytes 8192 | tf_op jit(solution)/shard_map/all_to_all | solution.py:108
  27.2 8.9 %all-to-all-start.5 = ((f32[4,8,2]{0,2,1:T(2,128)}), f32[4,8,2]{0,2,1:T(2,128)S(1)}, u32[]{:S(2)}, u32[]{:S(2)}) async-start(f32[4,8,2]{0,2,1:T(2,128)} %copy.23), calls=%async_computation.5 | async-start | bytes 16384 | tf_op jit(solution)/shard_map/all_to_all | solution.py:100
  36.1 54.5 %all-to-all-start.1 = ((f32[4,8,2]{0,2,1:T(2,128)}), f32[4,8,2]{0,2,1:T(2,128)S(1)}, u32[]{:S(2)}, u32[]{:S(2)}) async-start(f32[4,8,2]{0,2,1:T(2,128)} %copy.18), calls=%async_computation.1 | async-start | bytes 16384 | tf_op jit(solution)/shard_map/all_to_all | solution.py:107
  90.6 15.8 %all-to-all-start.2 = ((f32[4,8,2,512]{3,2,1,0:T(2,128)}), f32[4,8,2,512]{3,2,1,0:T(2,128)S(1)}, u32[]{:S(2)}, u32[]{:S(2)}) async-start(f32[4,8,2,512]{3,2,1,0:T(2,128)} %reshape.178), calls=%async_computation.2 | async-start | bytes 262144 | tf_op jit(solution)/shard_map/all_to_all | solution.py:94
  107.0 10.1 %all-to-all-start.3 = ((f32[4,8,2,512]{3,2,0,1:T(2,128)}), f32[4,8,2,512]{3,2,0,1:T(2,128)S(1)}, u32[]{:S(2)}, u32[]{:S(2)}) async-start(f32[4,8,2,512]{3,2,0,1:T(2,128)} %copy.20), calls=%async_computation.3 | async-start | bytes 262144 | tf_op jit(solution)/shard_map/all_to_all | solution.py:93
where the time goes:
time: 119 us; the launch traced here: 118 us
  blocking collectives  40.5 us (34%)
  other arithmetic  25.5 us (21%)
  starting transfers between devices  25.4 us (21%)
  waiting for transfers between devices  16.3 us (14%)
  local copies, waits for them, and re-layouts  6.49 us (5%)
  matrix products  3.31 us (3%)
    all_gather x1, blocking collectives, on_device(): hub_table = lax.all_gather(hub_feats, ('role', 'dom'), axis=0, tiled=True)  40.5 us
    scatter-add x1, other arithmetic, add_block(): node_sums.at[block_targets].add(picked)  11.6 us
    scatter-add x1, other arithmetic, add_block(): node_degree.at[block_targets].add(1.0)  7.61 us
    all_to_all x1, waiting for transfers between devices, on_device(): lax.all_to_all(lax.all_to_all(outgoing[0], 'role', split_axis=0, concat_a...  5.94 us
    all_to_all x1, waiting for transfers between devices, on_device(): lax.all_to_all(lax.all_to_all(outgoing[1], 'role', split_axis=0, concat_a...  4.84 us
    all_to_all x1, starting transfers between devices, on_device(): lax.all_to_all(outgoing[1], 'role', split_axis=0, concat_axis=0, tiled=True)  4.15 us
    ppermute x1, starting transfers between devices, extended(): lax.ppermute(lax.slice_in_dim(block, 0, width, axis=dim), axis, backward)  4.09 us
    all_to_all x1, waiting for transfers between devices, on_device(): lax.all_to_all(outgoing[2], 'role', split_axis=0, concat_axis=0, tiled=True)  3.94 us
  transfers between devices with their start and end apart: 8, of which 4 were waited for; matrix products, arithmetic and copies ran while one was open for 26% of the time, Pallas kernels for 0%

commit v1 on v0

--- a/solution.py
+++ b/solution.py
@@ -5,6 +5,18 @@
 from jax.sharding import PartitionSpec as P
 
 epsilon = 1e-06
+
+
+def collect(shard, axis, dim):
+    ways, here = (lax.axis_size(axis), lax.axis_index(axis))
+    grown, reach = (shard, 1)
+    while reach < ways:
+        theirs = lax.ppermute(grown, axis, [(d, d ^ reach) for d in range(ways)])
+        mine_first = jnp.concatenate([grown, theirs], axis=dim)
+        theirs_first = jnp.concatenate([theirs, grown], axis=dim)
+        grown = jnp.where(here & reach == 0, mine_first, theirs_first)
+        reach = 2 * reach
+    return grown
 
 
 def extended(block, sides, width):
@@ -47,7 +59,7 @@
     exports = node_feats[bound_rows[0]]
     bound_size = exports.shape[0]
     widened = extended(exports, (("dom", 0),), bound_size)
-    hub_table = lax.all_gather(hub_feats, ("role", "dom"), axis=0, tiled=True)
+    hub_table = collect(hub_feats, ("role", "dom"), 0)
     source_table = jnp.concatenate(
         [node_feats, widened[:bound_size], widened[2 * bound_size :], hub_table], axis=0
     )

time: 119 us -> 82.2 us (0.69)
  blocking collectives: 40.5 us -> 0 us
  starting transfers between devices: 25.4 us -> 32.9 us
  waiting for transfers between devices: 16.3 us -> 13.1 us
    all_gather x1 -> x0, blocking collectives: 40.5 us -> none  [on_device(): hub_table = lax.all_gather(hub_feats, ('role', 'dom'), axis=0, tiled=True)]
    all_to_all x1, waiting for transfers between devices: 5.94 us -> 0.01 us  [on_device(): lax.all_to_all(lax.all_to_all(outgoing[0], 'role', split_axis=0, concat_a...]
    ppermute x0 -> x5, starting transfers between devices: none -> 5 us  [collect(): theirs = lax.ppermute(grown, axis, [(d, d ^ reach) for d in range(ways)])]
    ppermute x0 -> x5, waiting for transfers between devices: none -> 3.62 us  [collect(): theirs = lax.ppermute(grown, axis, [(d, d ^ reach) for d in range(ways)])]
    all_to_all x1, waiting for transfers between devices: 0.01 us -> 2.62 us  [on_device(): lax.all_to_all(outgoing[0], 'role', split_axis=0, concat_axis=0, tiled=True)]
    all_to_all x1, waiting for transfers between devices: 3.94 us -> 1.89 us  [on_device(): lax.all_to_all(outgoing[2], 'role', split_axis=0, concat_axis=0, tiled=True)]
    all_to_all x1, waiting for transfers between devices: 1.58 us -> 0.01 us  [on_device(): lax.all_to_all(outgoing[1], 'role', split_axis=0, concat_axis=0, tiled=True)]
    all_to_all x1, starting transfers between devices: 3.37 us -> 4.87 us  [on_device(): lax.all_to_all(lax.all_to_all(outgoing[0], 'role', split_axis=0, concat_a...]
  transfers between devices with their start and end apart: 8 -> 13, of which waited for: 4 -> 4; matrix products, arithmetic and copies ran while one was open for 26% -> 38% of each run, Pallas kernels for 0% -> 0%
where the time goes in v1:
time: 82.2 us; the launch traced here: 81.6 us
  starting transfers between devices  32.9 us (40%)
  other arithmetic  25.6 us (31%)
  waiting for transfers between devices  13.1 us (16%)
  local copies, waits for them, and re-layouts  6.46 us (8%)
  matrix products  2.62 us (3%)
  between operations  0.98 us (1%)
    scatter-add x1, other arithmetic, add_block(): node_sums.at[block_targets].add(picked)  11.6 us
    scatter-add x1, other arithmetic, add_block(): node_degree.at[block_targets].add(1.0)  7.61 us
    ppermute x5, starting transfers between devices, collect(): theirs = lax.ppermute(grown, axis, [(d, d ^ reach) for d in range(ways)])  5 us
    all_to_all x1, waiting for transfers between devices, on_device(): lax.all_to_all(lax.all_to_all(outgoing[1], 'role', split_axis=0, concat_a...  4.91 us
    all_to_all x1, starting transfers between devices, on_device(): lax.all_to_all(lax.all_to_all(outgoing[0], 'role', split_axis=0, concat_a...  4.87 us
    all_to_all x1, starting transfers between devices, on_device(): lax.all_to_all(outgoing[2], 'role', split_axis=0, concat_axis=0, tiled=True)  4.19 us
    all_to_all x1, starting transfers between devices, on_device(): lax.all_to_all(outgoing[1], 'role', split_axis=0, concat_axis=0, tiled=True)  4.15 us
    ppermute x1, starting transfers between devices, extended(): lax.ppermute(lax.slice_in_dim(block, 0, width, axis=dim), axis, backward)  4.09 us
  transfers between devices with their start and end apart: 13, of which 4 were waited for; matrix products, arithmetic and copies ran while one was open for 38% of the time, Pallas kernels for 0%

profile of v1, /device:TPU:0, one launch (start us, length us, event | category | flops | bytes accessed | tf_op | source)
XLA Modules:
  0.0 81.6 jit_solution(15342850252344674569)
XLA Ops:
  0.6 0.0 copy-start.2
  0.6 0.0 copy-start
  0.7 0.0 copy-start.1
  0.7 0.0 copy-start.3
  0.7 0.0 copy-start.4
  0.7 0.0 copy-start.5
  0.7 0.0 copy-start.6
  0.7 0.7 fusion.18
  1.5 1.5 %gather_fusion = bf16[16,512]{1,0:T(8,128)(2,1)S(1)} fusion(bf16[128,512]{1,0:T(8,128)(2,1)} %param.9, s32[1024]{0:T(1024)S(1)} %pad_clamp_fusion.1), kind=kCustom, calls=%fused_computation | custom fusion | bytes 32832 | tf_op jit(solution)/shard_map/gather | solution.py:59
  3.0 0.5 collective-permute-start
  3.5 4.1 %collective-permute-start.1 = (bf16[16,512]{1,0:T(8,128)(2,1)S(1)}, bf16[16,512]{1,0:T(8,128)(2,1)S(1)}, u32[]{:S(2)}, u32[]{:S(2)}) collective-permute-start(bf16[16,512]{1,0:T(8,128)(2,1)S(1)} %gather_fusion), channel_id=1, source_target_pairs={{1,0},{2,1},{3,2},{4,3},{5,4},{6,5},{7,6},{0,7},{9,8},{10,9},{11,1... | collective-permute-start | bytes 49160 | tf_op jit(solution)/shard_map/ppermute | solution.py:31
  7.6 0.0 collective-permute-start.2
  7.6 0.7 fusion.19
  8.3 1.4 %scatter_custom_fusion.3 = f32[64]{0:T(128)S(1)} fusion(s32[128]{0:T(128)S(1)} %fusion.19, f32[128]{0:T(128)S(1)} %broadcast.143, f32[]{:T(128)} %constant.15.clone.1), kind=kCustom, calls=%fused_computation.55 | custom fusion | flops 128 | bytes 260 | tf_op jit(solution)/shard_map/scatter-add | solution.py:98
  9.7 0.1 reshape.180
  9.8 0.7 copy.22
  10.5 4.2 %all-to-all-start.4 = ((f32[4,8,2]{1,2,0:T(2,128)}), f32[4,8,2]{1,2,0:T(2,128)S(1)}, u32[]{:S(2)}, u32[]{:S(2)}) async-start(f32[4,8,2]{1,2,0:T(2,128)} %copy.22), calls=%async_computation.4 | async-start | bytes 8192 | tf_op jit(solution)/shard_map/all_to_all | solution.py:113
  14.6 1.3 %fusion.9 = f32[128,512]{1,0:T(8,128)S(1)} fusion(bf16[128,512]{1,0:T(8,128)(2,1)} %param.9, bf16[1024,512]{1,0:T(8,128)(2,1)} %param.11), kind=kOutput, calls=%fused_computation.20 | convolution fusion | flops 67108864 | bytes 917504 | tf_op jit(solution)/shard_map/dot_general | solution.py:38
  16.0 0.0 copy-done.2
  16.0 0.0 copy-done
  16.0 0.2 fusion.7
  16.3 0.0 collective-permute-done.2
  16.3 0.1 collective-permute-start.3
  16.4 3.6 %collective-permute-done.3 = bf16[8,512]{1,0:T(8,128)(2,1)S(1)} collective-permute-done((bf16[8,512]{1,0:T(8,128)(2,1)S(1)}, bf16[8,512]{1,0:T(8,128)(2,1)S(1)}, u32[]{:S(2)}, u32[]{:S(2)}) %collective-permute-start.3) | collective-permute-done | bytes 8224 | tf_op jit(solution)/shard_map/ppermute | solution.py:14
  20.0 0.8 collective-permute-start.4
  20.8 0.1 convert_element_type.31
  20.9 0.7 copy.17
  21.6 0.0 all-to-all-done.4
  21.6 4.2 %all-to-all-start = ((f32[4,8,2]{1,2,0:T(2,128)}), f32[4,8,2]{1,2,0:T(2,128)S(1)}, u32[]{:S(2)}, u32[]{:S(2)}) async-start(f32[4,8,2]{1,2,0:T(2,128)} %copy.17), calls=%async_computation | async-start | bytes 8192 | tf_op jit(solution)/shard_map/all_to_all | solution.py:120
  25.8 0.7 copy.23
  26.5 0.0 collective-permute-done.4
  26.5 2.1 %collective-permute-start.5 = (bf16[32,512]{1,0:T(8,128)(2,1)S(1)}, bf16[32,512]{1,0:T(8,128)(2,1)S(1)}, u32[]{:S(2)}, u32[]{:S(2)}) collective-permute-start(bf16[32,512]{1,0:T(8,128)(2,1)S(1)} %maximum_select_fusion.2), channel_id=1, source_target_pairs={{0,8},{1,9},{2,10},{3,11},{4,12},{5,13},{6,14},{7,15},{8,0},{9,1},... | collective-permute-start | bytes 98312 | tf_op jit(solution)/shard_map/ppermute | solution.py:14
  28.6 1.9 %all-to-all-done = f32[4,8,2]{1,2,0:T(2,128)S(1)} async-done(((f32[4,8,2]{1,2,0:T(2,128)}), f32[4,8,2]{1,2,0:T(2,128)S(1)}, u32[]{:S(2)}, u32[]{:S(2)}) %all-to-all-start) | async-done | bytes 288 | tf_op jit(solution)/shard_map/all_to_all | solution.py:120
  30.5 3.4 %all-to-all-start.5 = ((f32[4,8,2]{0,2,1:T(2,128)}), f32[4,8,2]{0,2,1:T(2,128)S(1)}, u32[]{:S(2)}, u32[]{:S(2)}) async-start(f32[4,8,2]{0,2,1:T(2,128)} %copy.23), calls=%async_computation.5 | async-start | bytes 16384 | tf_op jit(solution)/shard_map/all_to_all | solution.py:112
  33.9 0.7 copy.18
  34.6 4.9 %all-to-all-done.5 = f32[4,8,2]{0,2,1:T(2,128)S(1)} async-done(((f32[4,8,2]{0,2,1:T(2,128)}), f32[4,8,2]{0,2,1:T(2,128)S(1)}, u32[]{:S(2)}, u32[]{:S(2)}) %all-to-all-start.5) | async-done | bytes 288 | tf_op jit(solution)/shard_map/all_to_all | solution.py:112
  39.5 3.3 %all-to-all-start.1 = ((f32[4,8,2]{0,2,1:T(2,128)}), f32[4,8,2]{0,2,1:T(2,128)S(1)}, u32[]{:S(2)}, u32[]{:S(2)}) async-start(f32[4,8,2]{0,2,1:T(2,128)} %copy.18), calls=%async_computation.1 | async-start | bytes 16384 | tf_op jit(solution)/shard_map/all_to_all | solution.py:119
  42.8 0.0 copy-done.1
  42.9 2.0 %scatter_custom_fusion.2 = f32[64,512]{1,0:T(8,128)S(1)} fusion(s32[128]{0:T(128)S(1)} %fusion.19, f32[]{:T(128)} %constant.15.clone.1, bf16[128,512]{1,0:T(8,128)(2,1)S(1)} %copy-done.1, s32[1024]{0:T(1024)S(1)} %pad_clamp_fusion), kind=kCustom, calls=%fused_computation.23 | custom fusion | flops 131072 | bytes 266244 | tf_op jit(solution)/shard_map/scatter-add | solution.py:96
  44.8 0.7 reshape.178
  45.5 7.6 %scatter_custom_fusion.1 = f32[128]{0:T(128)S(1)} fusion(s32[1024]{0:T(1024)S(1)} %bitcast.26, f32[1024]{0:T(1024)S(1)} %broadcast.142, f32[]{:T(128)} %constant.15.clone.1), kind=kCustom, calls=%fused_computation.57 | custom fusion | flops 1024 | bytes 516 | tf_op jit(solution)/shard_map/while/body/eval_jaxpr/scatter-add | solution.py:75
  53.2 0.1 copy.24
  53.3 0.1 reshape.238
  53.4 0.0 all-to-all-done.1
  53.4 3.3 %all-to-all-start.2 = ((f32[4,8,2,512]{3,2,1,0:T(2,128)}), f32[4,8,2,512]{3,2,1,0:T(2,128)S(1)}, u32[]{:S(2)}, u32[]{:S(2)}) async-start(f32[4,8,2,512]{3,2,1,0:T(2,128)} %reshape.178), calls=%async_computation.2 | async-start | bytes 262144 | tf_op jit(solution)/shard_map/all_to_all | solution.py:106
  56.8 0.1 copy.19
  56.9 0.1 eq.35
  57.0 0.0 collective-permute-done.5
  57.0 2.1 %collective-permute-start.6 = (bf16[64,512]{1,0:T(8,128)(2,1)S(1)}, bf16[64,512]{1,0:T(8,128)(2,1)S(1)}, u32[]{:S(2)}, u32[]{:S(2)}) collective-permute-start(bf16[64,512]{1,0:T(8,128)(2,1)S(1)} %maximum_select_fusion.1), channel_id=1, source_target_pairs={{0,16},{1,17},{2,18},{3,19},{4,20},{5,21},{6,22},{7,23},{8,24},{9,... | collective-permute-start | bytes 196616 | tf_op jit(solution)/shard_map/ppermute | solution.py:14
  59.1 0.2 convolution_bitcast_fusion
  59.3 2.6 %all-to-all-done.2 = f32[4,8,2,512]{3,2,1,0:T(2,128)S(1)} async-done(((f32[4,8,2,512]{3,2,1,0:T(2,128)}), f32[4,8,2,512]{3,2,1,0:T(2,128)S(1)}, u32[]{:S(2)}, u32[]{:S(2)}) %all-to-all-start.2) | async-done | bytes 131104 | tf_op jit(solution)/shard_map/all_to_all | solution.py:106
  61.9 0.7 copy.20
  62.6 4.9 %all-to-all-start.3 = ((f32[4,8,2,512]{3,2,0,1:T(2,128)}), f32[4,8,2,512]{3,2,0,1:T(2,128)S(1)}, u32[]{:S(2)}, u32[]{:S(2)}) async-start(f32[4,8,2,512]{3,2,0,1:T(2,128)} %copy.20), calls=%async_computation.3 | async-start | bytes 262144 | tf_op jit(solution)/shard_map/all_to_all | solution.py:105
  67.4 0.0 collective-permute-done.6
  67.5 0.0 collective-permute-done
  67.5 0.0 collective-permute-done.1
  67.5 11.6 %scatter_custom_fusion = f32[128,512]{1,0:T(8,128)S(1)} fusion(s32[1024]{0:T(1024)S(1)} %bitcast.27, f32[]{:T(128)} %constant.15.clone.1, bf16[288,512]{1,0:T(8,128)(2,1)S(1)} %pad_maximum_fusion, s32[1024]{0:T(1024)S(1)} %broadcast_clamp_fusion), kind=kCustom, calls=%fused_computation.7 | custom fusion | flops 1048576 | bytes 561156 | tf_op jit(solution)/shard_map/while/body/eval_jaxpr/scatter-add | solution.py:75
  79.1 0.4 multiply_reduce_fusion
  79.5 0.8 multiply_convert_fusion
  80.2 0.0 all-to-all-done.3
  80.2 0.1 reshape.179
  80.3 0.3 fusion.4
  80.6 0.3 multiply_reduce_fusion.1
  80.9 0.7 multiply_convert_fusion.1
  (22 shorter events, 0.2 us)
Async XLA Ops:
  0.6 15.4 %copy-start.2 = (bf16[4,512]{1,0:T(4,128)(2,1)S(1)}, bf16[4,512]{1,0:T(4,128)(2,1)}, u32[]{:S(2)}) copy-start(bf16[4,512]{1,0:T(4,128)(2,1)} %param.10) | copy-start | bytes 12292
  0.6 15.4 %copy-start = (bf16[1024,512]{1,0:T(8,128)(2,1)S(1)}, bf16[1024,512]{1,0:T(8,128)(2,1)}, u32[]{:S(2)}) copy-start(bf16[1024,512]{1,0:T(8,128)(2,1)} %param.11) | copy-start | bytes 3145732
  0.7 42.2 %copy-start.1 = (bf16[128,512]{1,0:T(8,128)(2,1)S(1)}, bf16[128,512]{1,0:T(8,128)(2,1)}, u32[]{:S(2)}) copy-start(bf16[128,512]{1,0:T(8,128)(2,1)} %param.9) | copy-start | bytes 393220
  0.7 15.5 %copy-start.3 = (s32[1,1024]{1,0:T(1,128)S(1)}, s32[1,1024]{1,0:T(1,128)}, u32[]{:S(2)}) copy-start(s32[1,1024]{1,0:T(1,128)} %param.13) | copy-start | bytes 12292
  0.7 15.5 %copy-start.4 = (s32[1,1024]{1,0:T(1,128)S(1)}, s32[1,1024]{1,0:T(1,128)}, u32[]{:S(2)}) copy-start(s32[1,1024]{1,0:T(1,128)} %param.12) | copy-start | bytes 12292
  0.7 15.7 %copy-start.5 = (s32[1,128]{1,0:T(1,128)S(1)}, s32[1,128]{1,0:T(1,128)}, u32[]{:S(2)}) copy-start(s32[1,128]{1,0:T(1,128)} %param.15) | copy-start | bytes 1540
  0.7 20.1 %copy-start.6 = (s32[1,64]{1,0:T(1,128)S(1)}, s32[1,64]{1,0:T(1,128)}, u32[]{:S(2)}) copy-start(s32[1,64]{1,0:T(1,128)} %param.17) | copy-start | bytes 772
  3.0 64.5 %collective-permute-start = (bf16[16,512]{1,0:T(8,128)(2,1)S(1)}, bf16[16,512]{1,0:T(8,128)(2,1)S(1)}, u32[]{:S(2)}, u32[]{:S(2)}) collective-permute-start(bf16[16,512]{1,0:T(8,128)(2,1)S(1)} %gather_fusion), channel_id=1, source_target_pairs={{0,1},{1,2},{2,3},{3,4},{4,5},{5,6},{6,7},{7,0},{8,9},{9,10},{10,1... | collective-permute-start | bytes 49160 | tf_op jit(solution)/shard_map/ppermute | solution.py:28
  3.5 64.0 %collective-permute-start.1 = (bf16[16,512]{1,0:T(8,128)(2,1)S(1)}, bf16[16,512]{1,0:T(8,128)(2,1)S(1)}, u32[]{:S(2)}, u32[]{:S(2)}) collective-permute-start(bf16[16,512]{1,0:T(8,128)(2,1)S(1)} %gather_fusion), channel_id=1, source_target_pairs={{1,0},{2,1},{3,2},{4,3},{5,4},{6,5},{7,6},{0,7},{9,8},{10,9},{11,1... | collective-permute-start | bytes 49160 | tf_op jit(solution)/shard_map/ppermute | solution.py:31
  7.6 8.6 %collective-permute-start.2 = (bf16[4,512]{1,0:T(4,128)(2,1)}, bf16[4,512]{1,0:T(4,128)(2,1)S(1)}, u32[]{:S(2)}, u32[]{:S(2)}) collective-permute-start(bf16[4,512]{1,0:T(4,128)(2,1)} %param.10), channel_id=1, source_target_pairs={{0,1},{1,0},{2,3},{3,2},{4,5},{5,4},{6,7},{7,6},{8,9},{9,8},{10,11... | collective-permute-start | bytes 12296 | tf_op jit(solution)/shard_map/ppermute | solution.py:14
  10.5 11.1 %all-to-all-start.4 = ((f32[4,8,2]{1,2,0:T(2,128)}), f32[4,8,2]{1,2,0:T(2,128)S(1)}, u32[]{:S(2)}, u32[]{:S(2)}) async-start(f32[4,8,2]{1,2,0:T(2,128)} %copy.22), calls=%async_computation.4 | async-start | bytes 8192 | tf_op jit(solution)/shard_map/all_to_all | solution.py:113
  16.3 3.7 %collective-permute-start.3 = (bf16[8,512]{1,0:T(8,128)(2,1)S(1)}, bf16[8,512]{1,0:T(8,128)(2,1)S(1)}, u32[]{:S(2)}, u32[]{:S(2)}) collective-permute-start(bf16[8,512]{1,0:T(8,128)(2,1)S(1)} %maximum_select_fusion.4), channel_id=1, source_target_pairs={{0,2},{1,3},{2,0},{3,1},{4,6},{5,7},{6,4},{7,5},{8,10},{9,11},{10,... | collective-permute-start | bytes 24584 | tf_op jit(solution)/shard_map/ppermute | solution.py:14
  20.0 6.5 %collective-permute-start.4 = (bf16[16,512]{1,0:T(8,128)(2,1)S(1)}, bf16[16,512]{1,0:T(8,128)(2,1)S(1)}, u32[]{:S(2)}, u32[]{:S(2)}) collective-permute-start(bf16[16,512]{1,0:T(8,128)(2,1)S(1)} %maximum_select_fusion.3), channel_id=1, source_target_pairs={{0,4},{1,5},{2,6},{3,7},{4,0},{5,1},{6,2},{7,3},{8,12},{9,13},{10,... | collective-permute-start | bytes 49160 | tf_op jit(solution)/shard_map/ppermute | solution.py:14
  21.6 8.9 %all-to-all-start = ((f32[4,8,2]{1,2,0:T(2,128)}), f32[4,8,2]{1,2,0:T(2,128)S(1)}, u32[]{:S(2)}, u32[]{:S(2)}) async-start(f32[4,8,2]{1,2,0:T(2,128)} %copy.17), calls=%async_computation | async-start | bytes 8192 | tf_op jit(solution)/shard_map/all_to_all | solution.py:120
  26.5 30.5 %collective-permute-start.5 = (bf16[32,512]{1,0:T(8,128)(2,1)S(1)}, bf16[32,512]{1,0:T(8,128)(2,1)S(1)}, u32[]{:S(2)}, u32[]{:S(2)}) collective-permute-start(bf16[32,512]{1,0:T(8,128)(2,1)S(1)} %maximum_select_fusion.2), channel_id=1, source_target_pairs={{0,8},{1,9},{2,10},{3,11},{4,12},{5,13},{6,14},{7,15},{8,0},{9,1},... | collective-permute-start | bytes 98312 | tf_op jit(solution)/shard_map/ppermute | solution.py:14
  30.5 9.0 %all-to-all-start.5 = ((f32[4,8,2]{0,2,1:T(2,128)}), f32[4,8,2]{0,2,1:T(2,128)S(1)}, u32[]{:S(2)}, u32[]{:S(2)}) async-start(f32[4,8,2]{0,2,1:T(2,128)} %copy.23), calls=%async_computation.5 | async-start | bytes 16384 | tf_op jit(solution)/shard_map/all_to_all | solution.py:112
  39.5 13.9 %all-to-all-start.1 = ((f32[4,8,2]{0,2,1:T(2,128)}), f32[4,8,2]{0,2,1:T(2,128)S(1)}, u32[]{:S(2)}, u32[]{:S(2)}) async-start(f32[4,8,2]{0,2,1:T(2,128)} %copy.18), calls=%async_computation.1 | async-start | bytes 16384 | tf_op jit(solution)/shard_map/all_to_all | solution.py:119
  53.4 8.5 %all-to-all-start.2 = ((f32[4,8,2,512]{3,2,1,0:T(2,128)}), f32[4,8,2,512]{3,2,1,0:T(2,128)S(1)}, u32[]{:S(2)}, u32[]{:S(2)}) async-start(f32[4,8,2,512]{3,2,1,0:T(2,128)} %reshape.178), calls=%async_computation.2 | async-start | bytes 262144 | tf_op jit(solution)/shard_map/all_to_all | solution.py:106
  57.0 10.4 %collective-permute-start.6 = (bf16[64,512]{1,0:T(8,128)(2,1)S(1)}, bf16[64,512]{1,0:T(8,128)(2,1)S(1)}, u32[]{:S(2)}, u32[]{:S(2)}) collective-permute-start(bf16[64,512]{1,0:T(8,128)(2,1)S(1)} %maximum_select_fusion.1), channel_id=1, source_target_pairs={{0,16},{1,17},{2,18},{3,19},{4,20},{5,21},{6,22},{7,23},{8,24},{9,... | collective-permute-start | bytes 196616 | tf_op jit(solution)/shard_map/ppermute | solution.py:14
  62.6 17.7 %all-to-all-start.3 = ((f32[4,8,2,512]{3,2,0,1:T(2,128)}), f32[4,8,2,512]{3,2,0,1:T(2,128)S(1)}, u32[]{:S(2)}, u32[]{:S(2)}) async-start(f32[4,8,2,512]{3,2,0,1:T(2,128)} %copy.20), calls=%async_computation.3 | async-start | bytes 262144 | tf_op jit(solution)/shard_map/all_to_all | solution.py:105
